TPU v7x, 256 devices: a whole 4x4x8 slice. The times are simulated.
256 devices in a mesh: det: 64 (over x, z, core), row: 4 (over y).
Axes of the slice: x: 4, y: 4, z: 8, core: 2. Of those that a mesh axis runs over, the one named last changes fastest.
Arguments:
- images: bfloat16 [384, 3, 384, 384], P('det', None, 'row'), may hold values from -6 to 6
- warp_rows: bfloat16 [384, 3, 384, 384], P('det', None, 'row'), may hold values from -0.3125 to 0.3125
- warp_cols: bfloat16 [384, 3, 384, 384], P('det'), may hold values from -0.3125 to 0.3125
- psf_coef: float32 [384, 3, 21], P('det'), may hold values from -1.25 to 1.25
- taps: float32 [21, 21], replicated, may hold values from -1.25 to 1.25
- dest_patch: int32 [3456, 1], replicated, may hold values from 0 to 63; in each aligned block of 54 rows (0 to 53, 54 to 107, ...) at most 2 rows name the same one
- dest_block: int32 [3456], replicated, may hold values from 0 to 2
- weight_index: int32 [384, 3], replicated, may hold values from 0 to 7
- weight_table: float32 [8], replicated, may hold values from 0.25 to 4
- patch_home: int32 [64], replicated, may hold values from 0 to 63, each once
Outputs:
- difference: bfloat16 [384, 3, 384, 384], P('det', None, 'row')
- coadd: bfloat16 [64, 384, 384], P('det', 'row')
Inputs may be any that keep to these rules, and one draw needn't show every extreme that they name: `dest_patch`: within the 54 rows of one device (an aligned block of rows), no patch is named more than 2 times. `patch_home`: each position once.
All inputs are finite; a program needn't handle non-finite values.
Results may differ from a plain program's by a relative error of at most 0.0082.
Values may be sent and summed in bfloat16 or wider, within the bound.
A program may use at most 128 MiB of HBM per device.

v0:
```python
import jax
import jax.numpy as jnp
from jax import lax
from jax.sharding import PartitionSpec as P

TILE = 128


def extended(value, sides, width):
    for axis, dim in sides:
        size, length = (lax.axis_size(axis), value.shape[dim])
        up = [(i, (i + 1) % size) for i in range(size - 1)]
        down = [(j, i) for i, j in up]
        last = lax.slice_in_dim(value, length - width, length, axis=dim)
        first = lax.slice_in_dim(value, 0, width, axis=dim)
        before = lax.ppermute(last, axis, up)
        after = lax.ppermute(first, axis, down)
        value = jnp.concatenate([before, value, after], axis=dim)
    return value


def toeplitz_table(values, out_len, in_len):
    span_len = values.shape[1]
    offsets = jnp.arange(in_len)[None, :] - jnp.arange(out_len)[:, None]
    picks = (offsets[:, :, None] == jnp.arange(span_len)[None, None, :]).astype(jnp.float32)
    return jnp.einsum("oij,kj->koi", picks, values.astype(jnp.float32)).astype(jnp.bfloat16)


def per_device(
    images,
    warp_rows,
    warp_cols,
    psf_coef,
    taps,
    dest_patch,
    dest_block,
    weight_index,
    weight_table,
    patch_home,
):
    det_count, visit_count, band_rows, side_cols = images.shape
    kernel_count, tap_count = taps.shape
    reach = (tap_count - 1) // 2
    tile_cols = TILE
    tile_count = side_cols // tile_cols
    det_devices = lax.axis_size("det")
    my_index = lax.axis_index("det")
    image_count = det_count * visit_count
    piece_count = image_count * tile_count
    capacity = max(2, 2 * ((piece_count + det_devices - 1) // det_devices))
    slot_count = det_devices * capacity
    padded_rows = band_rows + 2 * reach
    col_warped = jnp.einsum(
        "dvbs,dvst->dvbt", images, warp_cols, preferred_element_type=jnp.float32
    ).astype(jnp.bfloat16)
    warped = jnp.einsum(
        "dvbr,dvrs->dvbs",
        warp_rows,
        lax.all_gather(col_warped, "row", axis=2, tiled=True),
        preferred_element_type=jnp.float32,
    ).astype(jnp.bfloat16)
    padded = extended(warped, (("row", 2),), reach)
    taps_half = taps.astype(jnp.bfloat16)
    col_table = toeplitz_table(taps_half, tile_cols, tile_cols + 2 * reach)
    tiles_in = padded.reshape(image_count, padded_rows, side_cols)
    coef_rows = psf_coef.reshape(image_count, kernel_count)

    def match_image(inputs):
        tile_image, coef_row = inputs
        widened = jnp.pad(tile_image, ((0, 0), (reach, reach)))
        windows = jnp.stack(
            [
                widened[
                    :, column_tile * tile_cols : column_tile * tile_cols + tile_cols + 2 * reach
                ]
                for column_tile in range(tile_count)
            ],
            axis=1,
        )
        conv_cols = jnp.einsum(
            "rtw,kcw->krtc", windows, col_table, preferred_element_type=jnp.float32
        ).astype(jnp.bfloat16)
        conv_cols = conv_cols.reshape(kernel_count, padded_rows, side_cols)
        scaled = (coef_row[:, None] * taps).astype(jnp.bfloat16)
        row_table = toeplitz_table(scaled, band_rows, padded_rows)
        return jnp.einsum("kbr,krs->bs", row_table, conv_cols, preferred_element_type=jnp.float32)

    matched = lax.map(match_image, (tiles_in, coef_rows))
    level_count = weight_table.shape[0]
    level_onehot = (weight_index[:, :, None] == jnp.arange(level_count)[None, None, :]).astype(
        jnp.float32
    )
    weight_all = jnp.sum(level_onehot * weight_table[None, None, :], axis=2)
    weight_mine = lax.dynamic_slice_in_dim(weight_all, my_index * det_count, det_count, 0).reshape(
        image_count
    )
    weighted = (
        (weight_mine[:, None, None] * matched)
        .astype(jnp.bfloat16)
        .reshape(image_count, band_rows, tile_count, tile_cols)
    )
    patch_count = patch_home.shape[0]
    patch_ids = dest_patch[:, 0]
    owner_all = jnp.sum(
        jnp.where(patch_ids[:, None] == jnp.arange(patch_count)[None, :], patch_home[None, :], 0),
        axis=1,
    )
    owner_grid = owner_all.reshape(det_devices, piece_count)
    earlier = jnp.arange(piece_count)[None, :] < jnp.arange(piece_count)[:, None]
    rank_grid = jnp.sum(
        ((owner_grid[:, :, None] == owner_grid[:, None, :]) & earlier[None]).astype(jnp.int32),
        axis=2,
    )
    slot_grid = owner_grid * capacity + rank_grid
    slot_mine = lax.dynamic_slice_in_dim(slot_grid, my_index, 1, 0)[0]
    send_pick = (
        (jnp.arange(slot_count)[:, None] == slot_mine[None, :])
        .astype(jnp.bfloat16)
        .reshape(slot_count, image_count, tile_count)
    )
    weight_pieces = jnp.repeat(weight_all.reshape(-1), tile_count)
    to_mine = owner_all == my_index
    block_onehot = (dest_block[:, None] == jnp.arange(tile_count)[None, :]).astype(jnp.float32)
    denominator = jnp.sum(
        jnp.where(to_mine[:, None], block_onehot * weight_pieces[:, None], 0.0), axis=0
    )
    source_slot = jnp.arange(
        det_devices * piece_count
    ) // piece_count * capacity + rank_grid.reshape(-1)
    slot_onehot = (
        (source_slot[:, None] == jnp.arange(slot_count)[None, :]) & to_mine[:, None]
    ).astype(jnp.float32)
    gather_matrix = jnp.einsum("iq,is->qs", block_onehot, slot_onehot).astype(jnp.bfloat16)
    outgoing = jnp.einsum(
        "spq,pbqc->sbc", send_pick, weighted, preferred_element_type=jnp.float32
    ).astype(jnp.bfloat16)
    received = lax.all_to_all(outgoing, "det", split_axis=0, concat_axis=0, tiled=True)
    numerator = jnp.einsum(
        "qs,sbc->bqc", gather_matrix, received, preferred_element_type=jnp.float32
    )
    template = (numerator / jnp.maximum(denominator, 1.0)[None, :, None]).astype(jnp.bfloat16)
    coadd_band = template.reshape(1, band_rows, side_cols)
    returned = jnp.einsum(
        "qs,bqc->sbc", gather_matrix, template, preferred_element_type=jnp.float32
    ).astype(jnp.bfloat16)
    arrived = lax.all_to_all(returned, "det", split_axis=0, concat_axis=0, tiled=True)
    local_template = jnp.einsum(
        "spq,sbc->pbqc", send_pick, arrived, preferred_element_type=jnp.float32
    )
    difference = (
        matched.reshape(image_count, band_rows, tile_count, tile_cols) - local_template
    ).astype(jnp.bfloat16)
    difference = difference.reshape(det_count, visit_count, band_rows, side_cols)
    return (difference, coadd_band)


def solution(mesh):
    placed = (
        P("det", None, "row", None),
        P("det", None, "row", None),
        P("det", None, None, None),
        P("det", None, None),
        P(),
        P(),
        P(),
        P(),
        P(),
        P(),
    )
    return jax.shard_map(
        per_device,
        mesh=mesh,
        in_specs=placed,
        out_specs=(P("det", None, "row", None), P("det", "row", None)),
        check_vma=False,
    )
```

profile of v0, /device:TPU:1, one launch (start us, length us, event | category | flops | bytes accessed | tf_op | source)
XLA Modules:
  0.0 490.7 jit_solution(14183806398760456192)
XLA Ops:
  8.5 4.7 convolution_convert_fusion.3
  15.2 62.1 %all-gather.2.cloned.1.call-done = bf16[6,3,384,384]{3,2,1,0:T(8,128)(2,1)} async-done(((bf16[6,3,96,384]{3,2,1,0:T(8,128)(2,1)}), bf16[6,3,384,384]{3,2,1,0:T(8,128)(2,1)}) %all-gather.2.cloned.1.call-update) | async-done | bytes 5308432 | tf_op jit(solution)/shard_map/all_gather | solution.py:59
  77.3 3.6 fusion.26
  81.0 2.7 collective-permute-start
  87.8 3.8 collective-permute-done.1
  93.4 198.1 %while.12 = (s32[]{:T(128)}, f32[18,96,384]{2,1,0:T(8,128)}, f32[18,21]{1,0:T(8,128)S(1)}, f32[21,21]{1,0:T(8,128)S(1)}, bf16[18,116,384]{2,1,0:T(8,128)(2,1)}, /*index=5*/bf16[21,128,148]{1,2,0:T(8,128)(2,1)}, s32[]{:T(128)}) while((s32[]{:T(128)}, f32[18,96,384]{2,1,0:T(8,128)}, f32[18,21]{1,0:T(8,128)S(1)}, f32[21,21]{1,0:T(8,128)S(1)}, ...), condition=%wide.region_1.2_spmd, body=%wide.region_0.1_spmd.sunk | while | flops 468033056 | bytes 10274817 | solution.py:88
  95.7 3.2 convert_bitcast_fusion.2
  98.9 3.0 copy.109
  101.9 2.5 fusion.84
  106.7 3.2 convert_bitcast_fusion.2
  109.9 3.0 copy.109
  117.7 3.2 convert_bitcast_fusion.2
  120.9 3.0 copy.109
  123.9 2.5 fusion.84
  128.7 3.2 convert_bitcast_fusion.2
  131.9 3.0 copy.109
  134.9 2.5 fusion.84
  139.7 3.2 convert_bitcast_fusion.2
  142.9 3.0 copy.109
  150.7 3.2 convert_bitcast_fusion.2
  153.9 3.0 copy.109
  161.7 3.2 convert_bitcast_fusion.2
  164.9 3.0 copy.109
  167.9 2.5 fusion.84
  172.7 3.2 convert_bitcast_fusion.2
  175.9 3.0 copy.109
  183.7 3.2 convert_bitcast_fusion.2
  186.9 3.0 copy.109
  189.9 2.5 fusion.84
  194.7 3.2 convert_bitcast_fusion.2
  197.9 3.0 copy.109
  200.9 2.5 fusion.84
  205.7 3.2 convert_bitcast_fusion.2
  208.9 3.0 copy.109
  216.7 3.2 convert_bitcast_fusion.2
  219.9 3.0 copy.109
  222.9 2.5 fusion.84
  227.7 3.2 convert_bitcast_fusion.2
  230.9 3.0 copy.109
  238.7 3.2 convert_bitcast_fusion.2
  241.9 3.0 copy.109
  244.9 2.5 fusion.84
  249.7 3.2 convert_bitcast_fusion.2
  252.9 3.0 copy.109
  255.9 2.5 fusion.84
  260.7 3.2 convert_bitcast_fusion.2
  263.9 3.0 copy.109
  267.0 2.5 fusion.84
  271.7 3.2 convert_bitcast_fusion.2
  274.9 3.0 copy.109
  278.0 2.5 fusion.84
  282.7 3.2 convert_bitcast_fusion.2
  285.9 3.0 copy.109
  289.0 2.5 fusion.84
  291.5 3.1 multiply_convert_fusion.1
  294.5 3.6 reshape.134
  300.1 3.7 copy.71
  303.8 12.1 %all-to-all-start = ((bf16[128,96,128]{2,1,0:T(8,128)(2,1)}), bf16[128,96,128]{2,1,0:T(8,128)(2,1)}, u32[]{:S(2)}, u32[]{:S(2)}) async-start(bf16[128,96,128]{2,1,0:T(8,128)(2,1)} %copy.71), calls=%async_computation | async-start | bytes 6291456 | tf_op jit(solution)/shard_map/all_to_all | solution.py:137
  318.4 71.0 %all-to-all-done = bf16[128,96,128]{2,1,0:T(8,128)(2,1)} async-done(((bf16[128,96,128]{2,1,0:T(8,128)(2,1)}), bf16[128,96,128]{2,1,0:T(8,128)(2,1)}, u32[]{:S(2)}, u32[]{:S(2)}) %all-to-all-start) | async-done | bytes 3145760 | tf_op jit(solution)/shard_map/all_to_all | solution.py:137
  389.4 2.8 fusion.34
  393.3 3.7 copy.74
  397.0 6.2 %all-to-all-start.1 = ((bf16[128,96,128]{2,1,0:T(8,128)(2,1)}), bf16[128,96,128]{2,1,0:T(8,128)(2,1)}, u32[]{:S(2)}, u32[]{:S(2)}) async-start(bf16[128,96,128]{2,1,0:T(8,128)(2,1)} %copy.74), calls=%async_computation.1 | async-start | bytes 6291456 | tf_op jit(solution)/shard_map/all_to_all | solution.py:146
  403.9 72.7 %all-to-all-done.1 = bf16[128,96,128]{2,1,0:T(8,128)(2,1)} async-done(((bf16[128,96,128]{2,1,0:T(8,128)(2,1)}), bf16[128,96,128]{2,1,0:T(8,128)(2,1)}, u32[]{:S(2)}, u32[]{:S(2)}) %all-to-all-start.1) | async-done | bytes 3145760 | tf_op jit(solution)/shard_map/all_to_all | solution.py:146
  476.7 3.3 fusion.15
  (175 shorter events, 75.0 us)
Async XLA Ops:
  7.2 1.3 copy-start
  7.2 6.1 %copy-start.9 = (f32[8]{0:T(128)S(1)}, f32[8]{0:T(128)}, u32[]{:S(2)}) copy-start(f32[8]{0:T(128)} %param.20) | copy-start | bytes 100
  7.2 6.1 %copy-start.7 = (s32[384,3]{0,1:T(4,128)S(1)}, s32[384,3]{0,1:T(4,128)}, u32[]{:S(2)}) copy-start(s32[384,3]{0,1:T(4,128)} %param.19) | copy-start | bytes 13828
  7.2 6.4 %copy-start.6 = (f32[6,3,21]{2,1,0:T(4,128)S(1)}, f32[6,3,21]{2,1,0:T(4,128)}, u32[]{:S(2)}) copy-start(f32[6,3,21]{2,1,0:T(4,128)} %param.15) | copy-start | bytes 4540
  7.2 6.4 %copy-start.5 = (s32[3456,1]{0,1:T(1,128)S(1)}, s32[3456,1]{0,1:T(1,128)}, u32[]{:S(2)}) copy-start(s32[3456,1]{0,1:T(1,128)} %param.17) | copy-start | bytes 41476
  7.2 6.5 %copy-start.8 = (s32[64]{0:T(128)S(1)}, s32[64]{0:T(128)}, u32[]{:S(2)}) copy-start(s32[64]{0:T(128)} %param.21) | copy-start | bytes 772
  7.2 70.1 %all-gather.2.cloned.1.call-start = ((), (), s32[]{:S(2)}) async-start(), calls=%async_computation.2 | async-start | bytes 6635520 | tf_op jit(solution)/shard_map/all_gather | solution.py:59
  13.2 64.1 %copy-start.2 = (bf16[6,3,96,384]{3,2,1,0:T(8,128)(2,1)S(1)}, bf16[6,3,96,384]{3,2,1,0:T(8,128)(2,1)}, u32[]{:S(2)}) copy-start(bf16[6,3,96,384]{3,2,1,0:T(8,128)(2,1)} %param.13) | copy-start | bytes 3981316
  15.2 69.8 %copy-start.3 = (f32[21,21]{1,0:T(8,128)S(1)}, f32[21,21]{1,0:T(8,128)}, u32[]{:S(2)}) copy-start(f32[21,21]{1,0:T(8,128)} %param.16) | copy-start | bytes 5296
  81.0 6.7 %collective-permute-start = (bf16[6,3,10,384]{3,2,1,0:T(8,128)(2,1)S(1)}, bf16[6,3,10,384]{3,2,1,0:T(8,128)(2,1)S(1)}, u32[]{:S(2)}, u32[]{:S(2)}) collective-permute-start(bf16[6,3,10,384]{3,2,1,0:T(8,128)(2,1)S(1)} %get-tuple-element.125), channel_id=1, source_target_pairs={{0,1},{1,2},{2,3},{4,5},{5,6},{6,7},{8,9},{9,10},{10,11},{12,13},{... | collective-permute-start | bytes 414728 | tf_op jit(solution)/shard_map/ppermute | solution.py:16
  83.7 7.9 %collective-permute-start.1 = (bf16[6,3,10,384]{3,2,1,0:T(8,128)(2,1)S(1)}, bf16[6,3,10,384]{3,2,1,0:T(8,128)(2,1)S(1)}, u32[]{:S(2)}, u32[]{:S(2)}) collective-permute-start(bf16[6,3,10,384]{3,2,1,0:T(8,128)(2,1)S(1)} %get-tuple-element.126), channel_id=1, source_target_pairs={{1,0},{2,1},{3,2},{5,4},{6,5},{7,6},{9,8},{10,9},{11,10},{13,12},{... | collective-permute-start | bytes 414728 | tf_op jit(solution)/shard_map/ppermute | solution.py:17
  303.8 13.3 %copy-start.4 = (s32[3456]{0:T(1024)S(1)}, s32[3456]{0:T(1024)}, u32[]{:S(2)}) copy-start(s32[3456]{0:T(1024)} %param.18) | copy-start | bytes 41476
  303.8 85.6 %all-to-all-start = ((bf16[128,96,128]{2,1,0:T(8,128)(2,1)}), bf16[128,96,128]{2,1,0:T(8,128)(2,1)}, u32[]{:S(2)}, u32[]{:S(2)}) async-start(bf16[128,96,128]{2,1,0:T(8,128)(2,1)} %copy.71), calls=%async_computation | async-start | bytes 6291456 | tf_op jit(solution)/shard_map/all_to_all | solution.py:137
  397.0 79.7 %all-to-all-start.1 = ((bf16[128,96,128]{2,1,0:T(8,128)(2,1)}), bf16[128,96,128]{2,1,0:T(8,128)(2,1)}, u32[]{:S(2)}, u32[]{:S(2)}) async-start(bf16[128,96,128]{2,1,0:T(8,128)(2,1)} %copy.74), calls=%async_computation.1 | async-start | bytes 6291456 | tf_op jit(solution)/shard_map/all_to_all | solution.py:146
  476.7 3.3 copy-start.1
Sparse Core Ops, SparseCore 0:
  13.4 63.8 all-gather.1
where the time goes:
time: 495 us; the launch traced here: 491 us
  waiting for transfers between devices  211 us (43%)
  matrix products  143 us (29%)
  local copies, waits for them, and re-layouts  92.9 us (19%)
  starting transfers between devices  22.4 us (5%)
  between operations  14.4 us (3%)
  other arithmetic  7.01 us (1%)
    all_to_all x1, waiting for transfers between devices, per_device(): lax.all_to_all(returned, 'det', split_axis=0, concat_axis=0, tiled=True)  72.7 us
    all_to_all x1, waiting for transfers between devices, per_device(): lax.all_to_all(outgoing, 'det', split_axis=0, concat_axis=0, tiled=True)  71 us
    all_gather x1, waiting for transfers between devices, per_device(): lax.all_gather(col_warped, 'row', axis=2, tiled=True)  62.1 us
    dot_general x18, matrix products, match_image(): jnp.einsum('rtw,kcw->krtc', windows, col_table, preferred_element_type=jn...  57.4 us
    convert_element_type x18, local copies, waits for them, and re-layouts, match_image(): conv_cols = jnp.einsum('rtw,kcw->krtc', windows, col_table, preferred_ele...  54.3 us
    dot_general x18, matrix products, match_image(): jnp.einsum('kbr,krs->bs', row_table, conv_cols, preferred_element_type=jn...  44.7 us
    dot_general x19, matrix products, toeplitz_table(): jnp.einsum('oij,kj->koi', picks, values.astype(jnp.float32))  22.1 us
    dynamic_slice x36, local copies, waits for them, and re-layouts, per_device(): matched = lax.map(match_image, (tiles_in, coef_rows))  18.7 us
  transfers between devices with their start and end apart: 5, of which 5 were waited for; matrix products, arithmetic and copies ran while one was open for 1% of the time, Pallas kernels for 0%

commit v1 on v0

--- a/solution.py
+++ b/solution.py
@@ -4,6 +4,22 @@
 from jax.sharding import PartitionSpec as P
 
 TILE = 128
+
+
+def product_in_turn(x, axis, dim, contribution):
+    size, index, width = (lax.axis_size(axis), lax.axis_index(axis), x.shape[dim])
+    right = [(i, (i + 1) % size) for i in range(size)]
+    behind = [(i, (i - 1) % size) for i in range(size)]
+    halfway = size // 2
+    from_left = from_right = x
+    total = contribution(x, index * width)
+    for lap in range(1, halfway + 1):
+        from_left = lax.ppermute(from_left, axis, right)
+        if lap < size - halfway:
+            from_right = lax.ppermute(from_right, axis, behind)
+            total = total + contribution(from_right, (index + lap) % size * width)
+        total = total + contribution(from_left, (index - lap) % size * width)
+    return total
 
 
 def extended(value, sides, width):
@@ -53,11 +69,16 @@
     col_warped = jnp.einsum(
         "dvbs,dvst->dvbt", images, warp_cols, preferred_element_type=jnp.float32
     ).astype(jnp.bfloat16)
-    warped = jnp.einsum(
-        "dvbr,dvrs->dvbs",
-        warp_rows,
-        lax.all_gather(col_warped, "row", axis=2, tiled=True),
-        preferred_element_type=jnp.float32,
+    warped = product_in_turn(
+        col_warped,
+        "row",
+        2,
+        lambda part, offset: jnp.einsum(
+            "dvbr,dvrs->dvbs",
+            lax.dynamic_slice_in_dim(warp_rows, offset, part.shape[2], axis=3),
+            part,
+            preferred_element_type=jnp.float32,
+        ),
     ).astype(jnp.bfloat16)
     padded = extended(warped, (("row", 2),), reach)
     taps_half = taps.astype(jnp.bfloat16)

time: 495 us -> 444 us (0.90)
  matrix products: 143 us -> 111 us
  waiting for transfers between devices: 211 us -> 197 us
  between operations: 14.4 us -> 0.97 us
  starting transfers between devices: 22.4 us -> 32 us
    all_gather x1 -> x0, waiting for transfers between devices: 62.1 us -> none  [per_device(): lax.all_gather(col_warped, 'row', axis=2, tiled=True)]
    ppermute x0 -> x3, waiting for transfers between devices: none -> 48.3 us  [the longest x2 48.3 us: product_in_turn(): from_left = lax.ppermute(from_left, axis, right)]
    dot_general x18, matrix products: 44.7 us -> 25.4 us  [match_image(): jnp.einsum('kbr,krs->bs', row_table, conv_cols, preferred_element_type=jn...]
    dot_general x19, matrix products: 22.1 us -> 7.15 us  [toeplitz_table(): jnp.einsum('oij,kj->koi', picks, values.astype(jnp.float32))]
    ppermute x0 -> x3, starting transfers between devices: none -> 5.29 us  [the longest x2 3.76 us: product_in_turn(): from_left = lax.ppermute(from_left, axis, right)]
  transfers between devices with their start and end apart: 5 -> 7, of which waited for: 5 -> 6; matrix products, arithmetic and copies ran while one was open for 1% -> 2% of each run, Pallas kernels for 0% -> 0%
where the time goes in v1:
time: 444 us; the launch traced here: 441 us
  waiting for transfers between devices  197 us (44%)
  matrix products  111 us (25%)
  local copies, waits for them, and re-layouts  91.6 us (21%)
  starting transfers between devices  32 us (7%)
  other arithmetic  7.94 us (2%)
    all_to_all x1, waiting for transfers between devices, per_device(): lax.all_to_all(returned, 'det', split_axis=0, concat_axis=0, tiled=True)  72.7 us
    all_to_all x1, waiting for transfers between devices, per_device(): lax.all_to_all(outgoing, 'det', split_axis=0, concat_axis=0, tiled=True)  71 us
    dot_general x18, matrix products, match_image(): jnp.einsum('rtw,kcw->krtc', windows, col_table, preferred_element_type=jn...  57.2 us
    convert_element_type x18, local copies, waits for them, and re-layouts, match_image(): conv_cols = jnp.einsum('rtw,kcw->krtc', windows, col_table, preferred_ele...  54.3 us
    ppermute x2, waiting for transfers between devices, product_in_turn(): from_left = lax.ppermute(from_left, axis, right)  48.3 us
    dot_general x18, matrix products, match_image(): jnp.einsum('kbr,krs->bs', row_table, conv_cols, preferred_element_type=jn...  25.4 us
    dynamic_slice x36, local copies, waits for them, and re-layouts, per_device(): matched = lax.map(match_image, (tiles_in, coef_rows))  18.5 us
    all_to_all x1, starting transfers between devices, per_device(): lax.all_to_all(outgoing, 'det', split_axis=0, concat_axis=0, tiled=True)  16.2 us
  transfers between devices with their start and end apart: 7, of which 6 were waited for; matrix products, arithmetic and copies ran while one was open for 2% of the time, Pallas kernels for 0%

profile of v1, /device:TPU:1, one launch (start us, length us, event | category | flops | bytes accessed | tf_op | source)
XLA Modules:
  0.0 440.6 jit_solution(10755922324129276715)
XLA Ops:
  0.7 4.2 convolution_convert_fusion.2
  4.9 2.2 collective-permute-start.1
  7.1 1.5 collective-permute-start
  10.3 25.2 %collective-permute-done.1 = bf16[6,3,96,384]{3,2,1,0:T(8,128)(2,1)} collective-permute-done((bf16[6,3,96,384]{3,2,1,0:T(8,128)(2,1)S(1)}, bf16[6,3,96,384]{3,2,1,0:T(8,128)(2,1)}, u32[]{:S(2)}, u32[]{:S(2)}) %collective-permute-start.1) | collective-permute-done | bytes 1327136 | tf_op jit(solution)/shard_map/ppermute | solution.py:17
  35.4 1.6 collective-permute-start.2
  38.3 1.9 fusion.46
  40.2 1.9 fusion.48
  42.1 23.2 %collective-permute-done.2 = bf16[6,3,96,384]{3,2,1,0:T(8,128)(2,1)} collective-permute-done((bf16[6,3,96,384]{3,2,1,0:T(8,128)(2,1)}, bf16[6,3,96,384]{3,2,1,0:T(8,128)(2,1)}, u32[]{:S(2)}, u32[]{:S(2)}) %collective-permute-start.2) | collective-permute-done | bytes 1327136 | tf_op jit(solution)/shard_map/ppermute | solution.py:17
  65.3 2.1 add_convert_fusion
  67.5 2.8 collective-permute-start.3
  70.3 1.5 collective-permute-start.4
  73.2 4.1 collective-permute-done.4
  77.3 2.7 pad_maximum_fusion
  80.0 164.2 %while.12 = (s32[]{:T(128)}, f32[18,96,384]{2,1,0:T(8,128)}, f32[18,21]{1,0:T(8,128)S(1)}, f32[21,21]{1,0:T(8,128)S(1)}, bf16[18,116,384]{2,1,0:T(8,128)(2,1)}, /*index=5*/bf16[21,128,148]{1,2,0:T(8,128)(2,1)}, s32[]{:T(128)}) while((s32[]{:T(128)}, f32[18,96,384]{2,1,0:T(8,128)}, f32[18,21]{1,0:T(8,128)S(1)}, f32[21,21]{1,0:T(8,128)S(1)}, ...), condition=%wide.region_1.2_spmd, body=%wide.region_0.1_spmd.sunk | while | flops 468033056 | bytes 10153205 | solution.py:109
  81.1 3.2 convert_bitcast_fusion.2
  84.3 3.0 copy.109
  90.2 3.2 convert_bitcast_fusion.2
  93.4 3.0 copy.109
  99.4 3.2 convert_bitcast_fusion.2
  102.5 3.0 copy.109
  108.5 3.2 convert_bitcast_fusion.2
  111.6 3.0 copy.109
  117.6 3.2 convert_bitcast_fusion.2
  120.8 3.0 copy.109
  126.7 3.2 convert_bitcast_fusion.2
  129.9 3.0 copy.109
  135.8 3.2 convert_bitcast_fusion.2
  139.0 3.0 copy.109
  144.9 3.2 convert_bitcast_fusion.2
  148.1 3.0 copy.109
  154.1 3.2 convert_bitcast_fusion.2
  157.3 3.0 copy.109
  163.2 3.2 convert_bitcast_fusion.2
  166.4 3.0 copy.109
  172.3 3.2 convert_bitcast_fusion.2
  175.5 3.0 copy.109
  181.4 3.2 convert_bitcast_fusion.2
  184.6 3.0 copy.109
  190.5 3.2 convert_bitcast_fusion.2
  193.7 3.0 copy.109
  199.6 3.2 convert_bitcast_fusion.2
  202.8 3.0 copy.109
  206.3 1.4 fusion.96
  208.8 3.2 convert_bitcast_fusion.2
  212.0 3.0 copy.109
  217.9 3.2 convert_bitcast_fusion.2
  221.1 3.0 copy.109
  224.5 1.4 fusion.96
  227.1 3.2 convert_bitcast_fusion.2
  230.2 3.0 copy.109
  236.2 3.2 convert_bitcast_fusion.2
  239.4 3.0 copy.109
  244.2 3.1 multiply_convert_fusion.1
  247.3 3.6 reshape.134
  250.9 1.9 bitcast_convert_fusion
  252.8 3.7 copy.71
  256.5 16.2 %all-to-all-start = ((bf16[128,96,128]{2,1,0:T(8,128)(2,1)}), bf16[128,96,128]{2,1,0:T(8,128)(2,1)}, u32[]{:S(2)}, u32[]{:S(2)}) async-start(bf16[128,96,128]{2,1,0:T(8,128)(2,1)} %copy.71), calls=%async_computation | async-start | bytes 6291456 | tf_op jit(solution)/shard_map/all_to_all | solution.py:158
  275.2 71.0 %all-to-all-done = bf16[128,96,128]{2,1,0:T(8,128)(2,1)} async-done(((bf16[128,96,128]{2,1,0:T(8,128)(2,1)}), bf16[128,96,128]{2,1,0:T(8,128)(2,1)}, u32[]{:S(2)}, u32[]{:S(2)}) %all-to-all-start) | async-done | bytes 3145760 | tf_op jit(solution)/shard_map/all_to_all | solution.py:158
  346.2 2.8 fusion.33
  350.1 3.7 copy.74
  353.8 6.2 %all-to-all-start.1 = ((bf16[128,96,128]{2,1,0:T(8,128)(2,1)}), bf16[128,96,128]{2,1,0:T(8,128)(2,1)}, u32[]{:S(2)}, u32[]{:S(2)}) async-start(bf16[128,96,128]{2,1,0:T(8,128)(2,1)} %copy.74), calls=%async_computation.1 | async-start | bytes 6291456 | tf_op jit(solution)/shard_map/all_to_all | solution.py:167
  360.7 72.7 %all-to-all-done.1 = bf16[128,96,128]{2,1,0:T(8,128)(2,1)} async-done(((bf16[128,96,128]{2,1,0:T(8,128)(2,1)}), bf16[128,96,128]{2,1,0:T(8,128)(2,1)}, u32[]{:S(2)}, u32[]{:S(2)}) %all-to-all-start.1) | async-done | bytes 3145760 | tf_op jit(solution)/shard_map/all_to_all | solution.py:167
  433.5 3.3 fusion.15
  438.3 2.3 reshape.136
  (179 shorter events, 58.9 us)
Async XLA Ops:
  0.6 37.1 %copy-start = (bf16[6,3,96,384]{3,2,1,0:T(8,128)(2,1)S(1)}, bf16[6,3,96,384]{3,2,1,0:T(8,128)(2,1)}, u32[]{:S(2)}) copy-start(bf16[6,3,96,384]{3,2,1,0:T(8,128)(2,1)} %param.13) | copy-start | bytes 3981316
  0.6 8.0 %copy-start.2 = (f32[21,21]{1,0:T(8,128)S(1)}, f32[21,21]{1,0:T(8,128)}, u32[]{:S(2)}) copy-start(f32[21,21]{1,0:T(8,128)} %param.16) | copy-start | bytes 5296
  4.8 5.3 %copy-start.5 = (f32[6,3,21]{2,1,0:T(4,128)S(1)}, f32[6,3,21]{2,1,0:T(4,128)}, u32[]{:S(2)}) copy-start(f32[6,3,21]{2,1,0:T(4,128)} %param.15) | copy-start | bytes 4540
  4.8 5.3 %copy-start.6 = (s32[384,3]{0,1:T(4,128)S(1)}, s32[384,3]{0,1:T(4,128)}, u32[]{:S(2)}) copy-start(s32[384,3]{0,1:T(4,128)} %param.19) | copy-start | bytes 13828
  4.8 5.3 %copy-start.8 = (f32[8]{0:T(128)S(1)}, f32[8]{0:T(128)}, u32[]{:S(2)}) copy-start(f32[8]{0:T(128)} %param.20) | copy-start | bytes 100
  4.9 32.4 %copy-start.4 = (s32[3456,1]{0,1:T(1,128)S(1)}, s32[3456,1]{0,1:T(1,128)}, u32[]{:S(2)}) copy-start(s32[3456,1]{0,1:T(1,128)} %param.17) | copy-start | bytes 41476
  4.9 32.4 %copy-start.7 = (s32[64]{0:T(128)S(1)}, s32[64]{0:T(128)}, u32[]{:S(2)}) copy-start(s32[64]{0:T(128)} %param.21) | copy-start | bytes 772
  4.9 30.6 %collective-permute-start.1 = (bf16[6,3,96,384]{3,2,1,0:T(8,128)(2,1)S(1)}, bf16[6,3,96,384]{3,2,1,0:T(8,128)(2,1)}, u32[]{:S(2)}, u32[]{:S(2)}) collective-permute-start(bf16[6,3,96,384]{3,2,1,0:T(8,128)(2,1)S(1)} %convolution_convert_fusion.2), channel_id=1, source_target_pairs={{0,1},{1,2},{2,3},{3,0},{4,5},{5,6},{6,7},{7,4},{8,9},{9,10},{10,1... | collective-permute-start | bytes 3981320 | tf_op jit(solution)/shard_map/ppermute | solution.py:17
  7.1 33.2 %collective-permute-start = (bf16[6,3,96,384]{3,2,1,0:T(8,128)(2,1)S(1)}, bf16[6,3,96,384]{3,2,1,0:T(8,128)(2,1)}, u32[]{:S(2)}, u32[]{:S(2)}) collective-permute-start(bf16[6,3,96,384]{3,2,1,0:T(8,128)(2,1)S(1)} %convolution_convert_fusion.2), channel_id=1, source_target_pairs={{0,3},{1,0},{2,1},{3,2},{4,7},{5,4},{6,5},{7,6},{8,11},{9,8},{10,9... | collective-permute-start | bytes 3981320 | tf_op jit(solution)/shard_map/ppermute | solution.py:19
  35.4 29.9 %collective-permute-start.2 = (bf16[6,3,96,384]{3,2,1,0:T(8,128)(2,1)}, bf16[6,3,96,384]{3,2,1,0:T(8,128)(2,1)}, u32[]{:S(2)}, u32[]{:S(2)}) collective-permute-start(bf16[6,3,96,384]{3,2,1,0:T(8,128)(2,1)} %collective-permute-done.1), channel_id=1, source_target_pairs={{0,1},{1,2},{2,3},{3,0},{4,5},{5,6},{6,7},{7,4},{8,9},{9,10},{10,1... | collective-permute-start | bytes 3981320 | tf_op jit(solution)/shard_map/ppermute | solution.py:17
  67.5 5.6 %collective-permute-start.3 = (bf16[6,3,10,384]{3,2,1,0:T(8,128)(2,1)S(1)}, bf16[6,3,10,384]{3,2,1,0:T(8,128)(2,1)S(1)}, u32[]{:S(2)}, u32[]{:S(2)}) collective-permute-start(bf16[6,3,10,384]{3,2,1,0:T(8,128)(2,1)S(1)} %get-tuple-element.125), channel_id=1, source_target_pairs={{0,1},{1,2},{2,3},{4,5},{5,6},{6,7},{8,9},{9,10},{10,11},{12,13},{... | collective-permute-start | bytes 414728 | tf_op jit(solution)/shard_map/ppermute | solution.py:32
  70.3 7.0 %collective-permute-start.4 = (bf16[6,3,10,384]{3,2,1,0:T(8,128)(2,1)S(1)}, bf16[6,3,10,384]{3,2,1,0:T(8,128)(2,1)}, u32[]{:S(2)}, u32[]{:S(2)}) collective-permute-start(bf16[6,3,10,384]{3,2,1,0:T(8,128)(2,1)S(1)} %get-tuple-element.126), channel_id=1, source_target_pairs={{1,0},{2,1},{3,2},{5,4},{6,5},{7,6},{9,8},{10,9},{11,10},{13,12},{... | collective-permute-start | bytes 414728 | tf_op jit(solution)/shard_map/ppermute | solution.py:33
  256.5 17.4 %copy-start.3 = (s32[3456]{0:T(1024)S(1)}, s32[3456]{0:T(1024)}, u32[]{:S(2)}) copy-start(s32[3456]{0:T(1024)} %param.18) | copy-start | bytes 41476
  256.5 89.7 %all-to-all-start = ((bf16[128,96,128]{2,1,0:T(8,128)(2,1)}), bf16[128,96,128]{2,1,0:T(8,128)(2,1)}, u32[]{:S(2)}, u32[]{:S(2)}) async-start(bf16[128,96,128]{2,1,0:T(8,128)(2,1)} %copy.71), calls=%async_computation | async-start | bytes 6291456 | tf_op jit(solution)/shard_map/all_to_all | solution.py:158
  353.8 79.7 %all-to-all-start.1 = ((bf16[128,96,128]{2,1,0:T(8,128)(2,1)}), bf16[128,96,128]{2,1,0:T(8,128)(2,1)}, u32[]{:S(2)}, u32[]{:S(2)}) async-start(bf16[128,96,128]{2,1,0:T(8,128)(2,1)} %copy.74), calls=%async_computation.1 | async-start | bytes 6291456 | tf_op jit(solution)/shard_map/all_to_all | solution.py:167
  433.5 3.3 copy-start.1
